TPU v7x, 256 devices: a whole 4x4x8 slice. The times are simulated.
256 devices in a mesh: grp: 2 (over core), dev: 128 (over x, y, z).
Axes of the slice: x: 4, y: 4, z: 8, core: 2. Of those that a mesh axis runs over, the one named last changes fastest.
Arguments:
- coarse_emb: bfloat16 [131072, 128], P('dev'), may hold values from -6 to 6
- req_ids: int32 [128, 2, 128, 16], P('dev', 'grp'), may hold values from 0 to 1023, as said below
- fine_slot: int32 [128, 2, 2048], P('dev', 'grp'), may hold values from 0 to 2047, as said below
- tiles: bfloat16 [4096, 2, 8, 128, 128], P('dev', 'grp'), may hold values from -0.125 to 0.125
- tile_cols: int32 [4096, 2, 8], P('dev', 'grp'), may hold values from 0 to 47
Outputs:
- smoothed: bfloat16 [524288, 128], P('dev')
Inputs may be any that keep to these rules, and one draw needn't show every extreme that they name: For each d, g and o only the first entries of req_ids[d, g, o] are requested, at most 16 of them, and for each d and g some owner o has all 16; the remaining entries are 0. fine_slot[d, g, i] = o * 16 + j always names a requested entry j of req_ids[d, g, o], and every requested entry is named by some fine node.
All inputs are finite; a program needn't handle non-finite values.
Results may differ from a plain program's by a relative error of at most 0.001.
Values may be sent and summed in bfloat16 or wider, within the bound.
No kernel may reach another device: no remote copies, remote signals or barrier semaphores. Data moves between devices by JAX's collectives and lax.ppermute only.
A program may use at most 64 MiB of HBM per device.

v0:
```python
import jax
import jax.numpy as jnp
from jax import lax
from jax.sharding import PartitionSpec as P


def with_halo(shard, sides, width):
    for axis, dim in sides:
        count, length = (lax.axis_size(axis), shard.shape[dim])
        up = [(i, (i + 1) % count) for i in range(count - 1)]
        down = [(j, i) for i, j in up]
        last = lax.slice_in_dim(shard, length - width, length, axis=dim)
        initial = lax.slice_in_dim(shard, 0, width, axis=dim)
        before = lax.ppermute(last, axis, up)
        after = lax.ppermute(initial, axis, down)
        shard = jnp.concatenate([before, shard, after], axis=dim)
    return shard


def per_device(coarse_emb, req_ids, fine_slot, tiles, tile_cols):
    owners = lax.axis_size("dev")
    slot_count = req_ids.shape[3]
    feature_dim = coarse_emb.shape[1]
    half_rows = fine_slot.shape[2]
    tile_rows = tiles.shape[3]
    fine_rows = tiles.shape[0] * tile_rows
    wanted_rows = jnp.take(
        coarse_emb, lax.all_to_all(req_ids, "dev", split_axis=2, concat_axis=0, tiled=True), axis=0
    )
    received = lax.all_to_all(wanted_rows, "dev", split_axis=0, concat_axis=2, tiled=True)
    slot_table = received.reshape(owners * slot_count, feature_dim)
    rows_per = min(512, half_rows)
    block_count = half_rows // rows_per
    columns = lax.iota(jnp.int32, owners * slot_count)

    def lift_block(slot_block):
        onehot = (slot_block[:, None] == columns[None, :]).astype(jnp.bfloat16)
        return jnp.dot(onehot, slot_table, preferred_element_type=jnp.float32).astype(jnp.bfloat16)

    lifted = lax.map(lift_block, fine_slot.reshape(block_count, rows_per)).reshape(
        half_rows, feature_dim
    )
    extended = with_halo(lifted, (("dev", 0),), half_rows)
    ext_blocks = extended.reshape(3 * half_rows // tile_rows, tile_rows, feature_dim)
    picked = ext_blocks[tile_cols[:, 0, :]]
    tile_sums = jnp.einsum(
        "rtij,rtjw->riw", tiles[:, 0], picked, preferred_element_type=jnp.float32
    )
    tile_sums = tile_sums.reshape(fine_rows, feature_dim)
    group = lax.axis_index("grp")
    own_part = lax.dynamic_update_slice(
        jnp.zeros((fine_rows, feature_dim), jnp.float32),
        lifted.astype(jnp.float32),
        (group * half_rows, 0),
    )
    partial_value = own_part - 0.5 * tile_sums
    summed = lax.psum(partial_value, "grp")
    return summed.astype(jnp.bfloat16)


def solution(mesh):
    return jax.shard_map(
        per_device,
        mesh=mesh,
        in_specs=(
            P("dev", None),
            P("dev", "grp", None, None),
            P("dev", "grp", None),
            P("dev", "grp", None, None, None),
            P("dev", "grp", None),
        ),
        out_specs=P("dev", None),
        check_vma=False,
    )
```

profile of v0, /device:TPU:1, one launch (start us, length us, event | category | flops | bytes accessed | tf_op | source)
XLA Modules:
  0.0 108.3 jit_solution(4448812067448210851)
XLA Ops:
  0.0 0.0 copy-start
  0.0 0.8 copy.10
  0.8 26.7 %all_to_all.24 = s32[1,1,128,16]{3,1,0,2:T(1,128)S(1)} all-to-all(s32[1,1,128,16]{3,1,0,2:T(1,128)S(1)} %copy.10), channel_id=1, replica_groups=mesh['grp'=2,'dev'=128] {'dev'}, dimensions={2} | all-to-all | bytes 16384 | tf_op jit(solution)/shard_map/all_to_all | solution.py:28
  27.6 0.1 reshape.137
  27.7 0.0 copy-done
  27.7 0.0 copy-start.3
  27.7 0.0 copy-start.4
  27.7 6.2 %gather_fusion = bf16[2048,128]{1,0:T(8,128)(2,1)S(1)} fusion(bf16[1024,128]{1,0:T(8,128)(2,1)S(1)} %copy-done, s32[2048]{0:T(1024)S(1)} %broadcast_clamp_fusion), kind=kCustom, calls=%fused_computation | custom fusion | bytes 1056768 | tf_op jit(solution)/shard_map/jit(_take)/gather | solution.py:27
  33.9 1.1 %broadcast_select_fusion = bf16[128,1,1,16,128]{4,3,2,1,0:T(8,128)(2,1)} fusion(bf16[128,1,1,16,128]{4,3,2,1,0:T(8,128)(2,1)S(1)} %bitcast.44, pred[128,16]{1,0:T(8,128)(4,1)S(1)} %compare_and_fusion), kind=kLoop, calls=%fused_computation.16 | loop fusion | flops 262144 | bytes 1050624 | tf_op jit(solution)/shard_map/jit(_take)/select_n | solution.py:27
  35.0 6.2 %all-to-all-start.1 = ((bf16[128,1,1,16,128]{4,3,2,1,0:T(8,128)(2,1)}), bf16[128,1,1,16,128]{4,3,2,1,0:T(8,128)(2,1)S(1)}, u32[]{:S(2)}, u32[]{:S(2)}) async-start(bf16[128,1,1,16,128]{4,3,2,1,0:T(8,128)(2,1)} %broadcast_select_fusion), calls=%async_computation.1 | async-start | bytes 1048576 | tf_op jit(solution)/shard_map/all_to_all | solution.py:30
  41.2 0.5 broadcast.89
  41.8 0.0 copy-done.3
  41.8 0.6 reduce.3
  42.4 0.0 copy-done.4
  42.4 0.1 copy.12
  42.5 0.1 reshape.145
  42.5 17.0 %all-to-all-done.1 = bf16[128,1,1,16,128]{4,3,2,1,0:T(8,128)(2,1)S(1)} async-done(((bf16[128,1,1,16,128]{4,3,2,1,0:T(8,128)(2,1)}), bf16[128,1,1,16,128]{4,3,2,1,0:T(8,128)(2,1)S(1)}, u32[]{:S(2)}, u32[]{:S(2)}) %all-to-all-start.1) | async-done | bytes 524320 | tf_op jit(solution)/shard_map/all_to_all | solution.py:30
  59.5 3.7 %while.11 = (s32[]{:T(128)}, bf16[4,512,128]{2,1,0:T(8,128)(2,1)S(1)}, s32[4,512]{1,0:T(4,128)S(1)}, bf16[2048,128]{1,0:T(8,128)(2,1)S(1)}, s32[]{:T(128)}) while((s32[]{:T(128)}, bf16[4,512,128]{2,1,0:T(8,128)(2,1)S(1)}, s32[4,512]{1,0:T(4,128)S(1)}, bf16[2048,128]{1,0:T(8,128)(2,1)S(1)}, s32[]{:T(128)}) %tuple.24), condition=%wide.region_1.2_spmd.clone, body=%wide.region_0.1_spmd.clone.sunk | while | flops 269549568 | bytes 661573 | solution.py:40
  59.5 0.9 fusion.16
  60.4 0.9 fusion.16
  61.4 0.9 fusion.16
  62.3 0.9 fusion.16
  63.2 2.5 %collective-permute-start = (bf16[2048,128]{1,0:T(8,128)(2,1)S(1)}, bf16[2048,128]{1,0:T(8,128)(2,1)S(1)}, u32[]{:S(2)}, u32[]{:S(2)}) collective-permute-start(bf16[2048,128]{1,0:T(8,128)(2,1)S(1)} %bitcast.45), channel_id=1, source_target_pairs={{0,1},{1,2},{2,3},{3,4},{4,5},{5,6},{6,7},{7,8},{8,9},{9,10},{10,1... | collective-permute-start | bytes 1572872 | tf_op jit(solution)/shard_map/ppermute | solution.py:14
  65.7 1.3 %collective-permute-start.1 = (bf16[2048,128]{1,0:T(8,128)(2,1)S(1)}, bf16[2048,128]{1,0:T(8,128)(2,1)S(1)}, u32[]{:S(2)}, u32[]{:S(2)}) collective-permute-start(bf16[2048,128]{1,0:T(8,128)(2,1)S(1)} %bitcast.46), channel_id=1, source_target_pairs={{1,0},{2,1},{3,2},{4,3},{5,4},{6,5},{7,6},{8,7},{9,8},{10,9},{11,1... | collective-permute-start | bytes 1572872 | tf_op jit(solution)/shard_map/ppermute | solution.py:15
  67.0 0.1 broadcast_in_dim.23
  67.2 0.1 convert_dynamic-update-slice_fusion
  67.3 0.0 copy-start.1
  67.3 6.6 %collective-permute-done = bf16[2048,128]{1,0:T(8,128)(2,1)S(1)} collective-permute-done((bf16[2048,128]{1,0:T(8,128)(2,1)S(1)}, bf16[2048,128]{1,0:T(8,128)(2,1)S(1)}, u32[]{:S(2)}, u32[]{:S(2)}) %collective-permute-start) | collective-permute-done | bytes 524320 | tf_op jit(solution)/shard_map/ppermute | solution.py:14
  73.8 0.0 copy-done.1
  73.9 3.9 %collective-permute-done.1 = bf16[2048,128]{1,0:T(8,128)(2,1)S(1)} collective-permute-done((bf16[2048,128]{1,0:T(8,128)(2,1)S(1)}, bf16[2048,128]{1,0:T(8,128)(2,1)S(1)}, u32[]{:S(2)}, u32[]{:S(2)}) %collective-permute-start.1) | collective-permute-done | bytes 524320 | tf_op jit(solution)/shard_map/ppermute | solution.py:15
  77.7 0.1 pad_maximum_fusion
  77.8 8.6 %gather_fusion.1 = bf16[256,128,128]{2,1,0:T(8,128)(2,1)} fusion(bf16[48,128,128]{2,1,0:T(8,128)(2,1)S(1)} %bitcast.42, s32[1024]{0:T(1024)S(1)} %pad_clamp_fusion), kind=kCustom, calls=%fused_computation.1 | custom fusion | bytes 16778240 | tf_op jit(solution)/shard_map/gather | solution.py:45
  86.4 0.0 copy-start.2
  86.4 8.3 %bitcast_multiply_fusion = f32[32,128,128]{1,2,0:T(8,128)S(1)} fusion(bf16[32,8,128,128]{3,2,1,0:T(8,128)(2,1)} %bitcast.43, bf16[32,1,8,128,128]{4,3,2,1,0:T(8,128)(2,1)} %param.10), kind=kOutput, calls=%fused_computation.13 | convolution fusion | flops 1074266112 | bytes 18874368 | tf_op jit(solution)/shard_map/rtij,rtjw->riw/dot_general | solution.py:46
  94.7 0.0 copy-done.2
  94.7 0.2 bitcast_subtract_fusion
  94.9 13.4 %all-reduce.1 = bf16[4096,128]{1,0:T(8,128)(2,1)} all-reduce(f32[4096,128]{1,0:T(8,128)S(1)} %bitcast_subtract_fusion), channel_id=1, replica_groups=mesh['grp'=2,'dev'=128] {'grp'}, use_global_device_ids=true, to_apply=%region_2.3 | all-reduce | flops 524288 | bytes 3145728 | tf_op jit(solution)/shard_map/psum | solution.py:57
  (11 shorter events, 0.1 us)
Async XLA Ops:
  0.0 27.7 %copy-start = (bf16[1024,128]{1,0:T(8,128)(2,1)S(1)}, bf16[1024,128]{1,0:T(8,128)(2,1)}, u32[]{:S(2)}) copy-start(bf16[1024,128]{1,0:T(8,128)(2,1)} %param.7) | copy-start | bytes 786436
  27.7 14.1 %copy-start.3 = (s32[1,1,2048]{2,1,0:T(1,128)S(1)}, s32[1,1,2048]{2,1,0:T(1,128)}, u32[]{:S(2)}) copy-start(s32[1,1,2048]{2,1,0:T(1,128)} %param.9) | copy-start | bytes 24580
  27.7 14.7 %copy-start.4 = (s32[32,1,8]{0,2,1:T(8,128)S(1)}, s32[32,1,8]{0,2,1:T(8,128)}, u32[]{:S(2)}) copy-start(s32[32,1,8]{0,2,1:T(8,128)} %param.11) | copy-start | bytes 3076
  35.0 24.5 %all-to-all-start.1 = ((bf16[128,1,1,16,128]{4,3,2,1,0:T(8,128)(2,1)}), bf16[128,1,1,16,128]{4,3,2,1,0:T(8,128)(2,1)S(1)}, u32[]{:S(2)}, u32[]{:S(2)}) async-start(bf16[128,1,1,16,128]{4,3,2,1,0:T(8,128)(2,1)} %broadcast_select_fusion), calls=%async_computation.1 | async-start | bytes 1048576 | tf_op jit(solution)/shard_map/all_to_all | solution.py:30
  63.2 10.6 %collective-permute-start = (bf16[2048,128]{1,0:T(8,128)(2,1)S(1)}, bf16[2048,128]{1,0:T(8,128)(2,1)S(1)}, u32[]{:S(2)}, u32[]{:S(2)}) collective-permute-start(bf16[2048,128]{1,0:T(8,128)(2,1)S(1)} %bitcast.45), channel_id=1, source_target_pairs={{0,1},{1,2},{2,3},{3,4},{4,5},{5,6},{6,7},{7,8},{8,9},{9,10},{10,1... | collective-permute-start | bytes 1572872 | tf_op jit(solution)/shard_map/ppermute | solution.py:14
  65.7 12.0 %collective-permute-start.1 = (bf16[2048,128]{1,0:T(8,128)(2,1)S(1)}, bf16[2048,128]{1,0:T(8,128)(2,1)S(1)}, u32[]{:S(2)}, u32[]{:S(2)}) collective-permute-start(bf16[2048,128]{1,0:T(8,128)(2,1)S(1)} %bitcast.46), channel_id=1, source_target_pairs={{1,0},{2,1},{3,2},{4,3},{5,4},{6,5},{7,6},{8,7},{9,8},{10,9},{11,1... | collective-permute-start | bytes 1572872 | tf_op jit(solution)/shard_map/ppermute | solution.py:15
  67.3 6.6 %copy-start.1 = (f32[4096,128]{1,0:T(8,128)}, f32[4096,128]{1,0:T(8,128)S(1)}, u32[]{:S(2)}) copy-start(f32[4096,128]{1,0:T(8,128)S(1)} %convert_dynamic-update-slice_fusion) | copy-start | bytes 6291460
  86.4 8.3 %copy-start.2 = (f32[4096,128]{1,0:T(8,128)S(1)}, f32[4096,128]{1,0:T(8,128)}, u32[]{:S(2)}) copy-start(f32[4096,128]{1,0:T(8,128)} %copy-done.1) | copy-start | bytes 6291460
where the time goes:
time: 109 us; the launch traced here: 108 us
  blocking collectives  40.1 us (37%)
  waiting for transfers between devices  27.4 us (25%)
  local copies, waits for them, and re-layouts  16.6 us (15%)
  matrix products  11.9 us (11%)
  starting transfers between devices  9.97 us (9%)
  other arithmetic  2.15 us (2%)
    all_to_all x1, blocking collectives, per_device(): lax.all_to_all(req_ids, 'dev', split_axis=2, concat_axis=0, tiled=True)  26.7 us
    all_to_all x1, waiting for transfers between devices, per_device(): lax.all_to_all(wanted_rows, 'dev', split_axis=0, concat_axis=2, tiled=True)  17 us
    psum x1, blocking collectives, per_device(): summed = lax.psum(partial_value, 'grp')  13.4 us
    gather x1, local copies, waits for them, and re-layouts, per_device(): picked = ext_blocks[tile_cols[:, 0, :]]  8.61 us
    dot_general x1, matrix products, per_device(): jnp.einsum('rtij,rtjw->riw', tiles[:, 0], picked, preferred_element_type=...  8.25 us
    ppermute x1, waiting for transfers between devices, with_halo(): before = lax.ppermute(last, axis, up)  6.57 us
    gather x1, local copies, waits for them, and re-layouts, per_device(): jnp.take(coarse_emb, lax.all_to_all(req_ids, 'dev', split_axis=2, concat_...  6.19 us
    all_to_all x1, starting transfers between devices, per_device(): lax.all_to_all(wanted_rows, 'dev', split_axis=0, concat_axis=2, tiled=True)  6.18 us
  transfers between devices with their start and end apart: 3, of which 3 were waited for; matrix products, arithmetic and copies ran while one was open for 1% of the time, Pallas kernels for 0%

commit v1 on v0

--- a/solution.py
+++ b/solution.py
@@ -54,7 +54,7 @@
         (group * half_rows, 0),
     )
     partial_value = own_part - 0.5 * tile_sums
-    summed = lax.psum(partial_value, "grp")
+    summed = lax.all_gather(partial_value, "grp").sum(axis=0)
     return summed.astype(jnp.bfloat16)
 
 

time: 109 us -> 138 us (1.27)
  waiting for transfers between devices: 27.4 us -> 50.8 us
  between operations: 0.18 us -> 13.6 us
  blocking collectives: 40.1 us -> 26.7 us
  other arithmetic: 2.15 us -> 7.37 us
    all_gather x0 -> x1, waiting for transfers between devices: none -> 23.8 us  [per_device(): summed = lax.all_gather(partial_value, 'grp').sum(axis=0)]
    psum x1 -> x0, blocking collectives: 13.4 us -> none  [per_device(): summed = lax.psum(partial_value, 'grp')]
    reduce_sum x0 -> x1, other arithmetic: none -> 3.77 us  [per_device(): summed = lax.all_gather(partial_value, 'grp').sum(axis=0)]
  transfers between devices with their start and end apart: 3 -> 4, of which waited for: 3 -> 4; matrix products, arithmetic and copies ran while one was open for 1% -> 1% of each run, Pallas kernels for 0% -> 0%
where the time goes in v1:
time: 138 us; the launch traced here: 137 us
  waiting for transfers between devices  50.8 us (37%)
  blocking collectives  26.7 us (19%)
  local copies, waits for them, and re-layouts  16.7 us (12%)
  between operations  13.6 us (10%)
  matrix products  11.9 us (9%)
  starting transfers between devices  10.2 us (7%)
  other arithmetic  7.37 us (5%)
    all_to_all x1, blocking collectives, per_device(): lax.all_to_all(req_ids, 'dev', split_axis=2, concat_axis=0, tiled=True)  26.7 us
    all_gather x1, waiting for transfers between devices, per_device(): summed = lax.all_gather(partial_value, 'grp').sum(axis=0)  23.8 us
    all_to_all x1, waiting for transfers between devices, per_device(): lax.all_to_all(wanted_rows, 'dev', split_axis=0, concat_axis=2, tiled=True)  16.7 us
    gather x1, local copies, waits for them, and re-layouts, per_device(): picked = ext_blocks[tile_cols[:, 0, :]]  8.63 us
    dot_general x1, matrix products, per_device(): jnp.einsum('rtij,rtjw->riw', tiles[:, 0], picked, preferred_element_type=...  8.25 us
    ppermute x1, waiting for transfers between devices, with_halo(): before = lax.ppermute(last, axis, up)  6.39 us
    gather x1, local copies, waits for them, and re-layouts, per_device(): jnp.take(coarse_emb, lax.all_to_all(req_ids, 'dev', split_axis=2, concat_...  6.19 us
    all_to_all x1, starting transfers between devices, per_device(): lax.all_to_all(wanted_rows, 'dev', split_axis=0, concat_axis=2, tiled=True)  6.18 us
  transfers between devices with their start and end apart: 4, of which 4 were waited for; matrix products, arithmetic and copies ran while one was open for 1% of the time, Pallas kernels for 0%

profile of v1, /device:TPU:1, one launch (start us, length us, event | category | flops | bytes accessed | tf_op | source)
XLA Modules:
  0.0 137.2 jit_solution(17537411295098364948)
XLA Ops:
  6.5 0.0 copy-start
  6.5 0.8 copy.10
  7.4 26.7 %all_to_all.24 = s32[1,1,128,16]{3,1,0,2:T(1,128)S(1)} all-to-all(s32[1,1,128,16]{3,1,0,2:T(1,128)S(1)} %copy.10), channel_id=1, replica_groups=mesh['grp'=2,'dev'=128] {'dev'}, dimensions={2} | all-to-all | bytes 16384 | tf_op jit(solution)/shard_map/all_to_all | solution.py:28
  34.1 0.1 reshape.137
  34.2 0.0 copy-done
  34.2 0.0 copy-start.3
  34.2 0.0 copy-start.4
  34.3 6.2 %gather_fusion = bf16[2048,128]{1,0:T(8,128)(2,1)S(1)} fusion(bf16[1024,128]{1,0:T(8,128)(2,1)S(1)} %copy-done, s32[2048]{0:T(1024)S(1)} %broadcast_clamp_fusion), kind=kCustom, calls=%fused_computation | custom fusion | bytes 1056768 | tf_op jit(solution)/shard_map/jit(_take)/gather | solution.py:27
  40.4 1.1 broadcast_select_fusion
  41.6 6.2 %all-to-all-start.1 = ((bf16[128,1,1,16,128]{4,3,2,1,0:T(8,128)(2,1)}), bf16[128,1,1,16,128]{4,3,2,1,0:T(8,128)(2,1)S(1)}, u32[]{:S(2)}, u32[]{:S(2)}) async-start(bf16[128,1,1,16,128]{4,3,2,1,0:T(8,128)(2,1)} %broadcast_select_fusion), calls=%async_computation.1 | async-start | bytes 1048576 | tf_op jit(solution)/shard_map/all_to_all | solution.py:30
  47.8 0.0 all-gather.3.cloned.1.call-start
  47.8 0.6 broadcast.89
  48.4 0.0 copy-done.3
  48.4 0.7 reduce.3
  49.1 0.0 copy-done.4
  49.2 0.1 copy.12
  49.2 0.1 reshape.145
  49.3 16.7 %all-to-all-done.1 = bf16[128,1,1,16,128]{4,3,2,1,0:T(8,128)(2,1)S(1)} async-done(((bf16[128,1,1,16,128]{4,3,2,1,0:T(8,128)(2,1)}), bf16[128,1,1,16,128]{4,3,2,1,0:T(8,128)(2,1)S(1)}, u32[]{:S(2)}, u32[]{:S(2)}) %all-to-all-start.1) | async-done | bytes 524320 | tf_op jit(solution)/shard_map/all_to_all | solution.py:30
  66.0 3.7 %while.11 = (s32[]{:T(128)}, bf16[4,512,128]{2,1,0:T(8,128)(2,1)S(1)}, s32[4,512]{1,0:T(4,128)S(1)}, bf16[2048,128]{1,0:T(8,128)(2,1)S(1)}, s32[]{:T(128)}) while((s32[]{:T(128)}, bf16[4,512,128]{2,1,0:T(8,128)(2,1)S(1)}, s32[4,512]{1,0:T(4,128)S(1)}, bf16[2048,128]{1,0:T(8,128)(2,1)S(1)}, s32[]{:T(128)}) %tuple.26), condition=%wide.region_1.2_spmd.clone, body=%wide.region_0.1_spmd.clone.sunk | while | flops 269549568 | bytes 661573 | solution.py:40
  66.0 0.9 fusion.16
  67.0 0.9 fusion.16
  67.9 0.9 fusion.16
  68.8 0.9 fusion.16
  69.8 2.5 %collective-permute-start = (bf16[2048,128]{1,0:T(8,128)(2,1)S(1)}, bf16[2048,128]{1,0:T(8,128)(2,1)S(1)}, u32[]{:S(2)}, u32[]{:S(2)}) collective-permute-start(bf16[2048,128]{1,0:T(8,128)(2,1)S(1)} %bitcast.47), channel_id=1, source_target_pairs={{0,1},{1,2},{2,3},{3,4},{4,5},{5,6},{6,7},{7,8},{8,9},{9,10},{10,1... | collective-permute-start | bytes 1572872 | tf_op jit(solution)/shard_map/ppermute | solution.py:14
  72.3 1.5 %collective-permute-start.1 = (bf16[2048,128]{1,0:T(8,128)(2,1)S(1)}, bf16[2048,128]{1,0:T(8,128)(2,1)S(1)}, u32[]{:S(2)}, u32[]{:S(2)}) collective-permute-start(bf16[2048,128]{1,0:T(8,128)(2,1)S(1)} %bitcast.48), channel_id=1, source_target_pairs={{1,0},{2,1},{3,2},{4,3},{5,4},{6,5},{7,6},{8,7},{9,8},{10,9},{11,1... | collective-permute-start | bytes 1572872 | tf_op jit(solution)/shard_map/ppermute | solution.py:15
  73.8 0.1 broadcast_in_dim.23
  73.9 0.1 convert_dynamic-update-slice_fusion
  74.0 0.0 copy-start.1
  74.0 6.4 %collective-permute-done = bf16[2048,128]{1,0:T(8,128)(2,1)S(1)} collective-permute-done((bf16[2048,128]{1,0:T(8,128)(2,1)S(1)}, bf16[2048,128]{1,0:T(8,128)(2,1)S(1)}, u32[]{:S(2)}, u32[]{:S(2)}) %collective-permute-start) | collective-permute-done | bytes 524320 | tf_op jit(solution)/shard_map/ppermute | solution.py:14
  80.4 0.0 copy-done.1
  80.4 3.9 %collective-permute-done.1 = bf16[2048,128]{1,0:T(8,128)(2,1)S(1)} collective-permute-done((bf16[2048,128]{1,0:T(8,128)(2,1)S(1)}, bf16[2048,128]{1,0:T(8,128)(2,1)S(1)}, u32[]{:S(2)}, u32[]{:S(2)}) %collective-permute-start.1) | collective-permute-done | bytes 524320 | tf_op jit(solution)/shard_map/ppermute | solution.py:15
  84.2 0.1 pad_maximum_fusion
  84.4 8.6 %gather_fusion.1 = bf16[256,128,128]{2,1,0:T(8,128)(2,1)} fusion(bf16[48,128,128]{2,1,0:T(8,128)(2,1)S(1)} %bitcast.43, s32[1024]{0:T(1024)S(1)} %pad_clamp_fusion), kind=kCustom, calls=%fused_computation.1 | custom fusion | bytes 16778240 | tf_op jit(solution)/shard_map/gather | solution.py:45
  93.0 0.0 copy-start.2
  93.0 8.3 %bitcast_multiply_fusion = f32[32,128,128]{1,2,0:T(8,128)S(1)} fusion(bf16[32,8,128,128]{3,2,1,0:T(8,128)(2,1)} %bitcast.44, bf16[32,1,8,128,128]{4,3,2,1,0:T(8,128)(2,1)} %param.10), kind=kOutput, calls=%fused_computation.13 | convolution fusion | flops 1074266112 | bytes 18874368 | tf_op jit(solution)/shard_map/rtij,rtjw->riw/dot_general | solution.py:46
  101.2 0.0 copy-done.2
  101.3 1.5 %bitcast_subtract_fusion = f32[4096,128]{1,0:T(8,128)} fusion(f32[4096,128]{1,0:T(8,128)S(1)} %copy-done.2, f32[32,128,128]{1,2,0:T(8,128)S(1)} %bitcast_multiply_fusion), kind=kLoop, calls=%fused_computation.12 | loop fusion | flops 524288 | bytes 6291456 | tf_op jit(solution)/shard_map/sub | solution.py:56
  102.8 0.0 all-gather.3.cloned.1.call-update
  102.8 23.8 %all-gather.3.cloned.1.call-done = f32[8192,128]{1,0:T(8,128)} async-done(((f32[4096,128]{1,0:T(8,128)}), f32[8192,128]{1,0:T(8,128)}) %all-gather.3.cloned.1.call-update) | async-done | bytes 4194320 | tf_op jit(solution)/shard_map/all_gather | solution.py:57
  126.6 3.8 %reduce_sum.9 = bf16[4096,128]{1,0:T(8,128)(2,1)} reduce(f32[2,4096,128]{2,1,0:T(8,128)} %bitcast.45, f32[]{:T(128)} %constant.13.clone.1), dimensions={0}, to_apply=%region_2.3 | reduce | flops 524288 | bytes 5242884 | tf_op jit(solution)/shard_map/reduce_sum | solution.py:57
  (11 shorter events, 0.1 us)
Async XLA Ops:
  6.5 27.7 %copy-start = (bf16[1024,128]{1,0:T(8,128)(2,1)S(1)}, bf16[1024,128]{1,0:T(8,128)(2,1)}, u32[]{:S(2)}) copy-start(bf16[1024,128]{1,0:T(8,128)(2,1)} %param.7) | copy-start | bytes 786436
  34.2 14.2 %copy-start.3 = (s32[1,1,2048]{2,1,0:T(1,128)S(1)}, s32[1,1,2048]{2,1,0:T(1,128)}, u32[]{:S(2)}) copy-start(s32[1,1,2048]{2,1,0:T(1,128)} %param.9) | copy-start | bytes 24580
  34.2 14.9 %copy-start.4 = (s32[32,1,8]{0,2,1:T(8,128)S(1)}, s32[32,1,8]{0,2,1:T(8,128)}, u32[]{:S(2)}) copy-start(s32[32,1,8]{0,2,1:T(8,128)} %param.11) | copy-start | bytes 3076
  41.6 24.5 %all-to-all-start.1 = ((bf16[128,1,1,16,128]{4,3,2,1,0:T(8,128)(2,1)}), bf16[128,1,1,16,128]{4,3,2,1,0:T(8,128)(2,1)S(1)}, u32[]{:S(2)}, u32[]{:S(2)}) async-start(bf16[128,1,1,16,128]{4,3,2,1,0:T(8,128)(2,1)} %broadcast_select_fusion), calls=%async_computation.1 | async-start | bytes 1048576 | tf_op jit(solution)/shard_map/all_to_all | solution.py:30
  47.8 78.8 %all-gather.3.cloned.1.call-start = ((), (), s32[]{:S(2)}) async-start(), calls=%async_computation.2 | async-start | bytes 6291456 | tf_op jit(solution)/shard_map/all_gather | solution.py:57
  69.8 10.6 %collective-permute-start = (bf16[2048,128]{1,0:T(8,128)(2,1)S(1)}, bf16[2048,128]{1,0:T(8,128)(2,1)S(1)}, u32[]{:S(2)}, u32[]{:S(2)}) collective-permute-start(bf16[2048,128]{1,0:T(8,128)(2,1)S(1)} %bitcast.47), channel_id=1, source_target_pairs={{0,1},{1,2},{2,3},{3,4},{4,5},{5,6},{6,7},{7,8},{8,9},{9,10},{10,1... | collective-permute-start | bytes 1572872 | tf_op jit(solution)/shard_map/ppermute | solution.py:14
  72.3 12.0 %collective-permute-start.1 = (bf16[2048,128]{1,0:T(8,128)(2,1)S(1)}, bf16[2048,128]{1,0:T(8,128)(2,1)S(1)}, u32[]{:S(2)}, u32[]{:S(2)}) collective-permute-start(bf16[2048,128]{1,0:T(8,128)(2,1)S(1)} %bitcast.48), channel_id=1, source_target_pairs={{1,0},{2,1},{3,2},{4,3},{5,4},{6,5},{7,6},{8,7},{9,8},{10,9},{11,1... | collective-permute-start | bytes 1572872 | tf_op jit(solution)/shard_map/ppermute | solution.py:15
  74.0 6.4 %copy-start.1 = (f32[4096,128]{1,0:T(8,128)}, f32[4096,128]{1,0:T(8,128)S(1)}, u32[]{:S(2)}) copy-start(f32[4096,128]{1,0:T(8,128)S(1)} %convert_dynamic-update-slice_fusion) | copy-start | bytes 6291460
  93.0 8.3 %copy-start.2 = (f32[4096,128]{1,0:T(8,128)S(1)}, f32[4096,128]{1,0:T(8,128)}, u32[]{:S(2)}) copy-start(f32[4096,128]{1,0:T(8,128)} %copy-done.1) | copy-start | bytes 6291460
Sparse Core Ops, SparseCore 0:
  102.9 23.6 all-gather.2
